TPU v7x, 128 devices: a whole 4x4x4 slice. The times are simulated.
128 devices in a mesh: req: 16 (over y, x), seq: 4 (over z), hid: 2 (over core).
Axes of the slice: x: 4, y: 4, z: 4, core: 2. Of those that a mesh axis runs over, the one named last changes fastest.
Arguments:
- tokens: bfloat16 [65536, 2048], P(('req', 'seq')), may hold values from -6 to 6
- attention_gain: bfloat16 [2048], replicated, may hold values from 0.099609375 to 1.8984375
- project_weight: bfloat16 [2048, 2048], P(None, 'hid'), may hold values from -0.125 to 0.125
- conv_weight: bfloat16 [4, 2048], P(None, 'hid'), may hold values from -3 to 3
- decay_down: bfloat16 [2048, 16], replicated, may hold values from -0.125 to 0.125
- decay_up: bfloat16 [16, 512], P(None, 'hid'), may hold values from -1.5 to 1.5
- decay_bias: float32 [512], P('hid'), may hold values from -2 to 10
- output_gate: bfloat16 [2048, 1024], P(None, 'hid'), may hold values from -0.125 to 0.125
- head_gain: bfloat16 [512], replicated, may hold values from 0.099609375 to 1.8984375
- output_weight: bfloat16 [1024, 2048], P('hid'), may hold values from -0.1875 to 0.1875
- mixer_gain: bfloat16 [2048], replicated, may hold values from 0.099609375 to 1.8984375
- gate_weight: bfloat16 [2048, 2816], P('req', 'hid'), may hold values from -0.125 to 0.125
- up_weight: bfloat16 [2048, 2816], P('req', 'hid'), may hold values from -0.125 to 0.125
- down_weight: bfloat16 [2816, 2048], P('hid', 'req'), may hold values from -0.109375 to 0.109375
- prompt_pages: int32 [16, 16], P('req'), may hold values from 0 to 64, as said below
- prompt_start: int32 [16, 16], P('req'), may hold values from 0 to 63, as said below
Outputs:
- hidden_out: bfloat16 [65536, 2048], P(('req', 'seq', 'hid'))
- page_states: bfloat16 [1024, 2, 256, 512], P(('req', 'seq'), 'hid')
- conv_edges: bfloat16 [1024, 3, 2048], P(('req', 'seq'), None, 'hid')
Inputs may be any that keep to these rules, and one draw needn't show every extreme that they name: `prompt_pages`: row r lists the page counts of the prompts of group r; 0 marks an unused slot; in every draw some group holds one prompt of all its 64 pages. `prompt_start`: the slots of a row that are used cover pages in increasing order without intersection and end by page 64; pages between prompts belong to none; an unused slot starts at page 64 - 1, and every draw has one.
All inputs are finite; a program needn't handle non-finite values.
Results may differ from a plain program's by a relative error of at most 0.014.
Values may be sent and summed in bfloat16 or wider, within the bound.
A program may use at most 192 MiB of HBM per device.

v0:
```python
import jax
import jax.numpy as jnp
from jax import lax
from jax.sharding import PartitionSpec as P

HK = 256
HV = 512
KCONV = 4
PAGE = 64
CONVW = 1024
EPSILON = 1e-06
TOP_PRECISION = lax.Precision.HIGHEST


def shifted(value, axis, steps):
    count = lax.axis_size(axis)
    first, last = (max(0, -steps), min(count, count - steps))
    return lax.ppermute(value, axis, [(source, source + steps) for source in range(first, last)])


def prefix_2(array, axis, join, neutral):
    place = lax.axis_index(axis)
    gathered = jax.tree.map(
        lambda a, kind: lax.all_gather(a.astype(kind), axis), array, (jnp.bfloat16, jnp.bfloat16)
    )
    state = jax.tree.map(lambda a, e: jnp.zeros_like(a) + jnp.asarray(e, a.dtype), array, neutral)

    def one(lap, state):
        return join(
            state,
            jax.tree.map(
                lambda a, own: lax.dynamic_index_in_dim(a, lap, 0, False).astype(own.dtype),
                gathered,
                array,
            ),
        )

    return lax.fori_loop(0, place, one, state)


def rms_scaled(values, scale_gain):
    values = values.astype(jnp.float32)
    return (
        values
        * lax.rsqrt(jnp.mean(values * values, axis=-1, keepdims=True) + EPSILON)
        * scale_gain.astype(jnp.float32)
    )


def page_segments(page_counts, starts, total_pages):
    position = jnp.arange(total_pages, dtype=jnp.int32)
    inside = (position[None, :] >= starts[:, None]) & (
        position[None, :] < starts[:, None] + page_counts[:, None]
    )
    labels = jnp.arange(1, page_counts.shape[0] + 1, dtype=jnp.int32)
    segment = jnp.sum(jnp.where(inside, labels[:, None], 0), axis=0) - 1
    earlier = jnp.concatenate([jnp.full((1,), -1, jnp.int32), segment[:-1]])
    return ((segment == earlier) & (segment >= 0)).astype(jnp.float32)


def short_conv(by_page, before, carried, conv_taps):
    kept_rows = before.astype(jnp.float32) * carried[:, None, None]
    widened = jnp.concatenate([kept_rows, by_page.astype(jnp.float32)], axis=1)
    tap_count = conv_taps.shape[0]
    length = by_page.shape[1]
    result = jnp.zeros(by_page.shape, jnp.float32)
    for offset in range(tap_count):
        result = (
            result
            + conv_taps[offset].astype(jnp.float32)
            * widened[:, tap_count - 1 - offset : tap_count - 1 - offset + length]
        )
    return result


def split_features(mixed_rows, key_width):
    query_rows = jax.nn.silu(mixed_rows[..., :key_width])
    key_rows = jax.nn.silu(mixed_rows[..., key_width : 2 * key_width]) * key_width ** (-0.5)
    value_matrix = mixed_rows[..., 2 * key_width :]
    return (
        query_rows.transpose(0, 2, 1, 3),
        key_rows.transpose(0, 2, 1, 3),
        value_matrix.transpose(0, 2, 1, 3),
    )


def page_block(query_rows, key_rows, value_matrix, decay_sum, carried):
    length = query_rows.shape[2]
    page_count = query_rows.shape[0]
    raised_rows = query_rows * jnp.exp(decay_sum)
    lowered = key_rows * jnp.exp(-decay_sum)
    scores = jnp.einsum("phik,phjk->phij", raised_rows, lowered, precision=TOP_PRECISION)
    rows_index = jnp.arange(length)
    causal = rows_index[:, None] >= rows_index[None, :]
    scores = jnp.where(causal[None, None], scores, 0.0)
    layer_output = jnp.einsum("phij,phjv->phiv", scores, value_matrix, precision=TOP_PRECISION)
    closing_sum = decay_sum[:, :, -1, :]
    weighted_rows = key_rows * jnp.exp(closing_sum[:, :, None, :] - decay_sum)
    page_terms = jnp.einsum("phte,phtb->pheb", weighted_rows, value_matrix, precision=TOP_PRECISION)
    through = jnp.cumsum(closing_sum, axis=0)
    resets = jnp.cumsum(1.0 - carried)
    pages = jnp.arange(page_count)
    valid = (pages[:, None] >= pages[None, :]) & (resets[:, None] == resets[None, :])
    spread = through[:, None] - through[None, :]
    spread = jnp.where(valid[:, :, None, None], spread, 0.0)
    weights = jnp.where(valid[:, :, None, None], jnp.exp(spread), 0.0)
    memories = jnp.einsum("pqhe,qheb->pheb", weights, page_terms, precision=TOP_PRECISION)
    previous = jnp.concatenate([jnp.zeros_like(memories[:1]), memories[:-1]], axis=0)
    previous = previous * carried[:, None, None, None]
    layer_output = layer_output + jnp.einsum(
        "phik,phkv->phiv", raised_rows, previous, precision=TOP_PRECISION
    )
    return (memories[-1], layer_output, memories)


def on_device(
    tokens,
    attention_gain,
    project_weight,
    conv_weight,
    decay_down,
    decay_up,
    decay_bias,
    output_gate,
    head_gain,
    output_weight,
    mixer_gain,
    gate_weight,
    up_weight,
    down_weight,
    prompt_pages,
    prompt_start,
):
    token_count = tokens.shape[0]
    page_count = token_count // PAGE
    local_heads = project_weight.shape[1] // CONVW
    rim_rows = KCONV - 1
    seq_index = lax.axis_index("seq")
    group_pages = page_count * lax.axis_size("seq")
    page_flags = page_segments(prompt_pages[0], prompt_start[0], group_pages)
    carried = lax.dynamic_slice_in_dim(page_flags, seq_index * page_count, page_count)
    normed = rms_scaled(tokens, attention_gain).astype(jnp.bfloat16)
    projected = jnp.dot(normed, project_weight, preferred_element_type=jnp.float32).astype(
        jnp.bfloat16
    )
    by_page = projected.reshape(page_count, PAGE, local_heads * CONVW)
    incoming = shifted(by_page[-1, PAGE - rim_rows :], "seq", 1)
    before = jnp.concatenate([incoming[None], by_page[:-1, PAGE - rim_rows :]], axis=0)
    mixed_rows = short_conv(by_page, before, carried, conv_weight).reshape(
        page_count, PAGE, local_heads, CONVW
    )
    query_rows, key_rows, value_matrix = split_features(mixed_rows, HK)
    gate_rows = lax.all_gather(gate_weight, "req", axis=0, tiled=True)
    up_rows = lax.all_gather(up_weight, "req", axis=0, tiled=True)
    down_columns = lax.all_gather(down_weight, "req", axis=1, tiled=True)
    gate_rows, query_rows = lax.optimization_barrier((gate_rows, query_rows))
    lowrank = jnp.dot(normed, decay_down, preferred_element_type=jnp.float32).astype(jnp.bfloat16)
    decay_log = (
        jax.nn.log_sigmoid(
            jnp.dot(lowrank, decay_up, preferred_element_type=jnp.float32) + decay_bias
        )
        / 16.0
    )
    decay_log = decay_log.reshape(page_count, PAGE, local_heads, HK).transpose(0, 2, 1, 3)
    decay_sum = jnp.cumsum(decay_log, axis=2)
    local_memory, outputs, memories = page_block(
        query_rows, key_rows, value_matrix, decay_sum, carried
    )
    totals = decay_sum[:, :, -1, :]
    through = jnp.cumsum(totals, axis=0)
    alive_mask = jnp.cumprod(carried)
    block_decay = alive_mask[-1] * jnp.exp(through[-1])

    def compose(earlier, latter):
        return (earlier[0] * latter[0], latter[0][..., None] * earlier[1] + latter[1])

    prefix = prefix_2(
        (block_decay, local_memory),
        "seq",
        compose,
        (jnp.ones_like(block_decay), jnp.zeros_like(local_memory)),
    )
    incoming_state = prefix[1]
    before_sum = through - totals
    extent_factor = alive_mask[:, None, None, None] * jnp.exp(decay_sum + before_sum[:, :, None, :])
    outputs = outputs + jnp.einsum(
        "dlof,lfg->dlog", query_rows * extent_factor, incoming_state, precision=TOP_PRECISION
    )
    memories = (
        memories + (alive_mask[:, None, None] * jnp.exp(through))[..., None] * incoming_state[None]
    )
    up_rows, outputs = lax.optimization_barrier((up_rows, outputs))
    attended = outputs.transpose(0, 2, 1, 3).reshape(token_count, local_heads, HV)
    normed_heads = rms_scaled(attended, head_gain)
    opening = jax.nn.silu(jnp.dot(normed, output_gate, preferred_element_type=jnp.float32)).reshape(
        token_count, local_heads, HV
    )
    gated_rows = (
        (normed_heads * opening).astype(jnp.bfloat16).reshape(token_count, local_heads * HV)
    )
    down_columns, gated_rows = lax.optimization_barrier((down_columns, gated_rows))
    partial_value = jnp.dot(gated_rows, output_weight, preferred_element_type=jnp.float32)
    half_rows = token_count // lax.axis_size("hid")
    row_start = lax.axis_index("hid") * half_rows
    mixed_sum = lax.psum(partial_value.astype(jnp.bfloat16), "hid").astype(jnp.float32)
    residual = (tokens.astype(jnp.float32) + mixed_sum).astype(jnp.bfloat16)
    feed_in = rms_scaled(residual, mixer_gain).astype(jnp.bfloat16)
    own_residual = lax.dynamic_slice_in_dim(residual, row_start, half_rows, 0)

    def widen(weight_rows):
        return jnp.dot(feed_in, weight_rows, preferred_element_type=jnp.float32)

    gate_part = widen(gate_rows)
    up_part = widen(up_rows)
    hidden = (jax.nn.silu(gate_part) * up_part).astype(jnp.bfloat16)
    partials = jnp.dot(hidden, down_columns, preferred_element_type=jnp.float32)
    feed_sum = lax.psum_scatter(
        partials.astype(jnp.bfloat16), "hid", scatter_dimension=0, tiled=True
    ).astype(jnp.float32)
    result = (own_residual.astype(jnp.float32) + feed_sum).astype(jnp.bfloat16)
    return (result, memories.astype(jnp.bfloat16), by_page[:, PAGE - rim_rows :])


def solution(mesh):
    return jax.shard_map(
        on_device,
        mesh=mesh,
        in_specs=(
            P(("req", "seq"), None),
            P(),
            P(None, "hid"),
            P(None, "hid"),
            P(),
            P(None, "hid"),
            P("hid"),
            P(None, "hid"),
            P(),
            P("hid", None),
            P(),
            P("req", "hid"),
            P("req", "hid"),
            P("hid", "req"),
            P("req", None),
            P("req", None),
        ),
        out_specs=(
            P(("req", "seq", "hid"), None),
            P(("req", "seq"), "hid", None, None),
            P(("req", "seq"), None, "hid"),
        ),
        check_vma=False,
    )
```

profile of v0, /device:TPU:1, one launch (start us, length us, event | category | flops | bytes accessed | tf_op | source)
XLA Modules:
  0.0 392.0 jit_solution(12662995687886767372)
XLA Ops:
  10.8 7.3 %convolution_convert_fusion.2 = bf16[1024,1024]{1,0:T(8,128)(2,1)S(1)} fusion(bf16[2048,1024]{1,0:T(8,128)(2,1)} %param.20, bf16[1024,2048]{1,0:T(8,128)(2,1)S(1)} %copy-done.7, f32[2048]{0:T(1024)S(1)} %convert_element_type.149, f32[1024]{0:T(1024)S(1)} %add_rsqrt_fusion.2), kind=kOutput, calls=%fused_computation.53 | convolution fusion | flops 4304404480 | bytes 10498048 | tf_op jit(solution)/shard_map/dot_general | solution.py:143
  19.4 4.4 %collective-permute-start = (bf16[3,1024]{1,0:T(4,128)(2,1)S(1)}, bf16[3,1024]{1,0:T(4,128)(2,1)S(1)}, u32[]{:S(2)}, u32[]{:S(2)}) collective-permute-start(bf16[3,1024]{1,0:T(4,128)(2,1)S(1)} %slice_bitcast_fusion.5), channel_id=1, source_target_pairs={{0,2},{2,4},{4,6},{1,3},{3,5},{5,7},{8,10},{10,12},{12,14},{9,11},... | collective-permute-start | bytes 18440 | tf_op jit(solution)/shard_map/ppermute | solution.py:18
  24.0 5.2 %fusion.37 = f32[1024,256]{1,0:T(8,128)} fusion(bf16[16,256]{1,0:T(8,128)(2,1)S(1)} %copy-done.18, bf16[2048,16]{0,1:T(8,128)(2,1)S(1)} %copy-done.17, f32[256]{0:T(256)S(1)} %copy-done.19, bf16[1024,2048]{1,0:T(8,128)(2,1)} %param.18, f32[2048]{0:T(1024)S(1)} %convert_element_type.149, f32[1024]{0:T(1024)S(1)} %add_rsqrt_fusion.2), kind=kOutput, calls=%fused_computation.60 | convolution fusion | flops 86523904 | bytes 5329920 | tf_op jit(solution)/shard_map/dot_general | solution.py:160
  32.6 4.1 %convert_element_type.152 = f32[16,64,1024]{2,1,0:T(8,128)} convert(bf16[16,64,1024]{2,1,0:T(8,128)(2,1)} %bitcast.123) | non-fusion elementwise | flops 1048576 | bytes 6291456 | tf_op jit(solution)/shard_map/convert_element_type | solution.py:63
  36.9 7.6 %fusion.15 = f32[16,64,1,1024]{3,1,0,2:T(8,128)S(1)} fusion(f32[16,64,1024]{2,1,0:T(8,128)} %convert_element_type.152, f32[16,3,1024]{2,1,0:T(4,128)S(1)} %convert_multiply_fusion.4, f32[1024]{0:T(1024)S(1)} %bitcast.130, f32[1024]{0:T(1024)S(1)} %bitcast.131, f32[1024]{0:T(1024)S(1)} %bitcast.129, f32[1024]{0:T(1024)S(1)} %bitcast.128), kind=kLoop, calls=%fused_computation.29 | loop fusion | flops 10485760 | bytes 8601600 | tf_op jit(solution)/shard_map/reshape | solution.py:149
  44.6 7.4 %fusion.30 = f32[16,256,512]{2,1,0:T(8,128)S(1)} fusion(f32[16,64,1,1024]{3,1,0,2:T(8,128)S(1)} %fusion.15, f32[16,1,64,256]{3,0,1,2:T(8,128)S(1)} %fusion.49, f32[16,256]{1,0:T(8,128)S(1)} %get-tuple-element.97), kind=kOutput, calls=%fused_computation.51 | convolution fusion | flops 1612447744 | bytes 12599296 | tf_op jit(solution)/shard_map/phte,phtb->pheb/dot_general | solution.py:99
  52.0 13.6 %fusion.20 = f32[16,1,256,512]{3,0,2,1:T(8,128)S(1)} fusion(f32[16,256,512]{2,1,0:T(8,128)S(1)} %fusion.30, f32[16,256]{0,1:T(8,128)S(1)} %bitcast.125, pred[16,16]{1,0:T(8,128)(4,1)S(1)} %fusion.72), kind=kOutput, calls=%fused_computation.38 | convolution fusion | flops 402849792 | bytes 16793856 | tf_op jit(solution)/shard_map/pqhe,qheb->pheb/dot_general | solution.py:107
  73.7 6.9 %all_gather.20 = bf16[4,1,256]{2,1,0:T(2,128)(2,1)S(1)} all-gather(bf16[1,1,256]{2,1,0:T(2,128)(2,1)S(1)} %fusion.74), channel_id=1, replica_groups=mesh['req'=16,'seq'=4,'hid'=2] {'seq'}, dimensions={0}, use_global_device_ids=true | all-gather | bytes 2560 | tf_op jit(solution)/shard_map/all_gather | solution.py:24
  83.1 8.6 %multiply_bitcast_fusion = f32[16,256,512]{2,0,1:T(8,128)} fusion(f32[15,1,256,512]{3,0,2,1:T(8,128)} %bitcast.119, f32[16]{0:T(128)S(1)} %get-tuple-element.95), kind=kLoop, calls=%fused_computation.19 | loop fusion | flops 2097152 | bytes 16252992 | tf_op jit(solution)/shard_map/reshape.33
  91.7 4.1 %all-gather.11.cloned.1.call-done = bf16[4,1,256,512]{3,2,1,0:T(8,128)(2,1)} async-done(((bf16[1,1,256,512]{3,2,1,0:T(8,128)(2,1)}), bf16[4,1,256,512]{3,2,1,0:T(8,128)(2,1)}) %all-gather.11.cloned.1.call-update) | async-done | bytes 1048592 | tf_op jit(solution)/shard_map/all_gather | solution.py:24
  96.0 62.0 %all-gather.9.cloned.1.call-done = bf16[2048,1408]{1,0:T(8,128)(2,1)} async-done(((bf16[128,1408]{1,0:T(8,128)(2,1)}), bf16[2048,1408]{1,0:T(8,128)(2,1)}) %all-gather.9.cloned.1.call-update) | async-done | bytes 5767184 | tf_op jit(solution)/shard_map/all_gather | solution.py:153
  158.0 4.7 %convolution_select_fusion = f32[16,64,64]{2,1,0:T(8,128)S(1)} fusion(f32[16,1,64,256]{3,2,0,1:T(8,128)} %multiply_bitcast_fusion.1, f32[16,1,64,256]{3,0,1,2:T(8,128)} %copy-done.5, pred[64,64]{1,0:T(8,128)(4,1)S(1)} %iota_compare_fusion, f32[16,64,1,1024]{3,1,0,2:T(8,128)} %copy-done.4), kind=kOutput, calls=%fused_computation.56 | convolution fusion | flops 203489280 | bytes 4460544 | tf_op jit(solution)/shard_map/phik,phjk->phij/dot_general | solution.py:92
  166.2 10.6 %fusion.7 = f32[16,64,512]{2,1,0:T(8,128)S(1)} fusion(f32[16,256,512]{2,0,1:T(8,128)S(1)} %copy-done.3, f32[16,1,64,256]{3,2,0,1:T(8,128)S(1)} %copy-done.8, f32[16,1,64,256]{3,0,1,2:T(8,128)S(1)} %copy-done.6), kind=kOutput, calls=%fused_computation.14 | convolution fusion | flops 1610874880 | bytes 12582912 | tf_op jit(solution)/shard_map/phik,phkv->phiv/dot_general | solution.py:110
  180.6 38.0 %all-gather.7.cloned.1.call-done = bf16[2048,1408]{1,0:T(8,128)(2,1)} async-done(((bf16[128,1408]{1,0:T(8,128)(2,1)}), bf16[2048,1408]{1,0:T(8,128)(2,1)}) %all-gather.7.cloned.1.call-update) | async-done | bytes 5767184 | tf_op jit(solution)/shard_map/all_gather | solution.py:154
  220.5 7.1 %fusion.25 = bf16[1024,512]{1,0:T(8,128)(2,1)} fusion(f32[16,1,64,512]{3,2,0,1:T(8,128)} %bitcast_add_fusion, f32[512]{0:T(512)S(1)} %convert_element_type.163, f32[1024]{0:T(1024)S(1)} %rsqrt.29, bf16[2048,512]{1,0:T(8,128)(2,1)} %param.25, bf16[1024,2048]{1,0:T(8,128)(2,1)} %param.18, f32[2048]{0:T(1024)S(1)} %convert_element_type.149, ...), kind=kOutput, calls=%fused_computation.45 | convolution fusion | flops 2160066560 | bytes 9455616 | tf_op jit(solution)/shard_map/dot_general | solution.py:195
  227.6 56.9 %all-gather.5.cloned.1.call-done = bf16[1408,2048]{1,0:T(8,128)(2,1)} async-done(((bf16[1408,128]{1,0:T(8,128)(2,1)}), bf16[1408,2048]{1,0:T(8,128)(2,1)}) %all-gather.5.cloned.1.call-update) | async-done | bytes 5767184 | tf_op jit(solution)/shard_map/all_gather | solution.py:155
  284.5 5.6 %convolution_convert_fusion.1 = bf16[1024,2048]{1,0:T(8,128)(2,1)} fusion(bf16[1024,512]{1,0:T(8,128)(2,1)} %fusion.25, bf16[512,2048]{1,0:T(8,128)(2,1)S(1)} %copy-done), kind=kOutput, calls=%fused_computation.37 | convolution fusion | flops 2149580800 | bytes 7340032 | tf_op jit(solution)/shard_map/dot_general | solution.py:202
  290.8 34.2 %all-reduce.3.cloned.1.call-done = bf16[1024,2048]{1,0:T(8,128)(2,1)} async-done(((bf16[1024,2048]{1,0:T(8,128)(2,1)}), bf16[1024,2048]{1,0:T(8,128)(2,1)}) %all-reduce.3.cloned.1.call-update) | async-done | bytes 4194320 | tf_op jit(solution)/shard_map/psum | solution.py:205
  325.0 5.5 %fusion = (f32[1024]{0:T(1024)S(1)}, bf16[1024,2048]{1,0:T(8,128)(2,1)S(1)}) fusion(bf16[1024,2048]{1,0:T(8,128)(2,1)} %all-reduce.3.cloned.1.call-done, bf16[1024,2048]{1,0:T(8,128)(2,1)} %param.18), kind=kLoop, calls=%fused_computation.7 | loop fusion | flops 14679040 | bytes 12587008 | tf_op jit(solution)/shard_map/reduce_sum | solution.py:45
  332.5 10.7 %fusion.34 = f32[1024,1408]{1,0:T(8,128)} fusion(bf16[2048,1408]{1,0:T(8,128)(2,1)} %all-gather.9.cloned.1.call-done, bf16[1024,2048]{1,0:T(8,128)(2,1)S(1)} %get-tuple-element.93, f32[2048]{0:T(1024)S(1)} %convert_element_type.170, f32[1024]{0:T(1024)S(1)} %add_rsqrt_fusion.1), kind=kOutput, calls=%fused_computation.57 | convolution fusion | flops 5913968640 | bytes 15740928 | tf_op jit(solution)/shard_map/dot_general | solution.py:211
  343.2 20.9 %convolution_convert_fusion = bf16[1024,2048]{1,0:T(8,128)(2,1)} fusion(bf16[1408,2048]{1,0:T(8,128)(2,1)} %all-gather.5.cloned.1.call-done, f32[1024,1408]{1,0:T(8,128)} %fusion.34, bf16[2048,1408]{1,0:T(8,128)(2,1)} %all-gather.7.cloned.1.call-done, bf16[1024,2048]{1,0:T(8,128)(2,1)} %copy-done.9, f32[2048]{0:T(1024)S(1)} %convert_element_type.170, ...), kind=kOutput, calls=%fused_computation.36 | convolution fusion | flops 11830296576 | bytes 25702400 | tf_op jit(solution)/shard_map/dot_general | solution.py:216
  370.0 4.5 %copy.75 = bf16[16,1,256,512]{3,2,1,0:T(8,128)(2,1)} copy(bf16[16,1,256,512]{3,0,2,1:T(8,128)(2,1)S(1)} %add_convert_fusion) | data formatting | bytes 8388608
  374.5 5.8 %reduce-scatter.2.cloned.1.call-done = bf16[512,2048]{1,0:T(8,128)(2,1)} async-done(((bf16[1024,2048]{1,0:T(8,128)(2,1)}), bf16[512,2048]{1,0:T(8,128)(2,1)}) %reduce-scatter.2.cloned.1.call-update) | async-done | bytes 2097168 | tf_op jit(solution)/shard_map/reduce_scatter | solution.py:217
  380.3 4.4 %add_convert_fusion.1 = bf16[512,2048]{1,0:T(8,128)(2,1)} fusion(bf16[512,2048]{1,0:T(8,128)(2,1)} %reduce-scatter.2.cloned.1.call-done, bf16[1024,2048]{1,0:T(8,128)(2,1)} %copy-done.9, s32[]{:T(128)S(6)} %select_n.46), kind=kLoop, calls=%fused_computation.35 | loop fusion | flops 4194304 | bytes 6291460 | tf_op jit(solution)/shard_map/convert_element_type | solution.py:220
  (98 shorter events, 37.1 us)
Async XLA Ops:
  7.2 277.4 %copy-start = (bf16[512,2048]{1,0:T(8,128)(2,1)S(1)}, bf16[512,2048]{1,0:T(8,128)(2,1)}, u32[]{:S(2)}) copy-start(bf16[512,2048]{1,0:T(8,128)(2,1)} %param.27) | copy-start | bytes 6291460
  7.2 3.3 copy-start.12
  7.2 88.6 %all-gather.11.cloned.1.call-start = ((), (), s32[]{:S(2)}) async-start(), calls=%async_computation.4 | async-start | bytes 1310720 | tf_op jit(solution)/shard_map/all_gather | solution.py:24
  7.2 3.6 copy-start.7
  10.8 13.0 %copy-start.14 = (s32[1,16]{1,0:T(1,128)S(1)}, s32[1,16]{1,0:T(1,128)}, u32[]{:S(2)}) copy-start(s32[1,16]{1,0:T(1,128)} %param.33) | copy-start | bytes 196
  10.8 13.0 %copy-start.16 = (s32[1,16]{1,0:T(1,128)S(1)}, s32[1,16]{1,0:T(1,128)}, u32[]{:S(2)}) copy-start(s32[1,16]{1,0:T(1,128)} %param.32) | copy-start | bytes 196
  10.8 13.2 %copy-start.11 = (bf16[4,1024]{1,0:T(4,128)(2,1)S(1)}, bf16[4,1024]{1,0:T(4,128)(2,1)}, u32[]{:S(2)}) copy-start(bf16[4,1024]{1,0:T(4,128)(2,1)} %param.21) | copy-start | bytes 24580
  10.8 13.2 %copy-start.17 = (bf16[2048,16]{0,1:T(8,128)(2,1)S(1)}, bf16[2048,16]{0,1:T(8,128)(2,1)}, u32[]{:S(2)}) copy-start(bf16[2048,16]{0,1:T(8,128)(2,1)} %param.22) | copy-start | bytes 196612
  10.8 13.2 %copy-start.18 = (bf16[16,256]{1,0:T(8,128)(2,1)S(1)}, bf16[16,256]{1,0:T(8,128)(2,1)}, u32[]{:S(2)}) copy-start(bf16[16,256]{1,0:T(8,128)(2,1)} %param.23) | copy-start | bytes 24580
  10.8 13.2 %copy-start.19 = (f32[256]{0:T(256)S(1)}, f32[256]{0:T(256)}, u32[]{:S(2)}) copy-start(f32[256]{0:T(256)} %param.24) | copy-start | bytes 3076
  19.4 17.3 %collective-permute-start = (bf16[3,1024]{1,0:T(4,128)(2,1)S(1)}, bf16[3,1024]{1,0:T(4,128)(2,1)S(1)}, u32[]{:S(2)}, u32[]{:S(2)}) collective-permute-start(bf16[3,1024]{1,0:T(4,128)(2,1)S(1)} %slice_bitcast_fusion.5), channel_id=1, source_target_pairs={{0,2},{2,4},{4,6},{1,3},{3,5},{5,7},{8,10},{10,12},{12,14},{9,11},... | collective-permute-start | bytes 18440 | tf_op jit(solution)/shard_map/ppermute | solution.py:18
  31.0 13.5 %copy-start.5 = (f32[16,1,64,256]{3,0,1,2:T(8,128)}, f32[16,1,64,256]{3,0,1,2:T(8,128)S(1)}, u32[]{:S(2)}) copy-start(f32[16,1,64,256]{3,0,1,2:T(8,128)S(1)} %fusion.49) | copy-start | bytes 3145732
  44.6 7.4 %copy-start.4 = (f32[16,64,1,1024]{3,1,0,2:T(8,128)}, f32[16,64,1,1024]{3,1,0,2:T(8,128)S(1)}, u32[]{:S(2)}) copy-start(f32[16,64,1,1024]{3,1,0,2:T(8,128)S(1)} %fusion.15) | copy-start | bytes 12582916
  52.0 21.1 %copy-start.15 = (bf16[512]{0:T(512)(128)(2,1)S(1)}, bf16[512]{0:T(512)(128)(2,1)}, u32[]{:S(2)}) copy-start(bf16[512]{0:T(512)(128)(2,1)} %param.26) | copy-start | bytes 3076
  65.6 3.2 copy-start.2
  70.1 87.9 %all-gather.9.cloned.1.call-start = ((), (), s32[]{:S(2)}) async-start(), calls=%async_computation.3 | async-start | bytes 6127616 | tf_op jit(solution)/shard_map/all_gather | solution.py:153
  70.9 147.7 %all-gather.7.cloned.1.call-start = ((), (), s32[]{:S(2)}) async-start(), calls=%async_computation.2 | async-start | bytes 6127616 | tf_op jit(solution)/shard_map/all_gather | solution.py:154
  71.6 212.9 %all-gather.5.cloned.1.call-start = ((), (), s32[]{:S(2)}) async-start(), calls=%async_computation.1 | async-start | bytes 6127616 | tf_op jit(solution)/shard_map/all_gather | solution.py:155
  72.2 252.8 %all-reduce.3.cloned.1.call-start = ((), (), s32[]{:S(2)}) async-start(), calls=%async_computation.5 | async-start | bytes 8388608 | tf_op jit(solution)/shard_map/psum | solution.py:205
  158.0 8.2 %copy-start.3 = (f32[16,256,512]{2,0,1:T(8,128)S(1)}, f32[16,256,512]{2,0,1:T(8,128)}, u32[]{:S(2)}) copy-start(f32[16,256,512]{2,0,1:T(8,128)} %multiply_bitcast_fusion) | copy-start | bytes 25165828
  158.0 8.2 %copy-start.6 = (f32[16,1,64,256]{3,0,1,2:T(8,128)S(1)}, f32[16,1,64,256]{3,0,1,2:T(8,128)}, u32[]{:S(2)}) copy-start(f32[16,1,64,256]{3,0,1,2:T(8,128)} %copy-done.5) | copy-start | bytes 3145732
  158.0 8.2 %copy-start.8 = (f32[16,1,64,256]{3,2,0,1:T(8,128)S(1)}, f32[16,1,64,256]{3,2,0,1:T(8,128)}, u32[]{:S(2)}) copy-start(f32[16,1,64,256]{3,2,0,1:T(8,128)} %multiply_bitcast_fusion.1) | copy-start | bytes 3145732
  290.2 90.2 %reduce-scatter.2.cloned.1.call-start = ((), (), s32[]{:S(2)}) async-start(), calls=%async_computation.6 | async-start | bytes 6291456 | tf_op jit(solution)/shard_map/reduce_scatter | solution.py:217
  370.0 14.8 %copy-start.1 = (bf16[512,2048]{1,0:T(8,128)(2,1)S(1)}, bf16[512,2048]{1,0:T(8,128)(2,1)}, u32[]{:S(2)}) copy-start(bf16[512,2048]{1,0:T(8,128)(2,1)} %param.27) | copy-start | bytes 6291460
  (3 other events, 4.0 us)
Sparse Core Ops, SparseCore 0:
  70.2 25.4 all-gather.10
  97.9 60.0 all-gather.8
  160.1 58.4 all-gather.6
  220.6 63.9 all-gather.4
  290.3 34.7 all-reduce.2
  364.2 16.0 reduce-scatter.1
where the time goes:
time: 398 us; the launch traced here: 392 us
  waiting for transfers between devices  203 us (51%)
  matrix products  100 us (25%)
  other arithmetic  45.1 us (11%)
  local copies, waits for them, and re-layouts  17 us (4%)
  between operations  15 us (4%)
  blocking collectives  6.9 us (2%)
  starting transfers between devices  4.61 us (1%)
    all_gather x1, waiting for transfers between devices, on_device(): gate_rows = lax.all_gather(gate_weight, 'req', axis=0, tiled=True)  62 us
    all_gather x1, waiting for transfers between devices, on_device(): down_columns = lax.all_gather(down_weight, 'req', axis=1, tiled=True)  56.9 us
    all_gather x1, waiting for transfers between devices, on_device(): up_rows = lax.all_gather(up_weight, 'req', axis=0, tiled=True)  38 us
    psum x1, waiting for transfers between devices, on_device(): lax.psum(partial_value.astype(jnp.bfloat16), 'hid').astype(jnp.float32)  34.2 us
    dot_general x1, matrix products, on_device(): partials = jnp.dot(hidden, down_columns, preferred_element_type=jnp.float32)  20.9 us
    dot_general x1, matrix products, page_block(): jnp.einsum('pqhe,qheb->pheb', weights, page_terms, precision=TOP_PRECISION)  13.6 us
    unnamed x43, local copies, waits for them, and re-layouts  12.8 us
    dot_general x1, matrix products, widen(): return jnp.dot(feed_in, weight_rows, preferred_element_type=jnp.float32)  10.7 us
  transfers between devices with their start and end apart: 7, of which 6 were waited for; matrix products, arithmetic and copies ran while one was open for 17% of the time, Pallas kernels for 0%

commit v1 on v0

--- a/solution.py
+++ b/solution.py
@@ -150,8 +150,13 @@
         page_count, PAGE, local_heads, CONVW
     )
     query_rows, key_rows, value_matrix = split_features(mixed_rows, HK)
-    gate_rows = lax.all_gather(gate_weight, "req", axis=0, tiled=True)
-    up_rows = lax.all_gather(up_weight, "req", axis=0, tiled=True)
+    gate_rows, up_rows = jnp.split(
+        lax.all_gather(
+            jnp.concatenate([gate_weight, up_weight], axis=1), "req", axis=0, tiled=True
+        ),
+        [gate_weight.shape[1]],
+        axis=1,
+    )
     down_columns = lax.all_gather(down_weight, "req", axis=1, tiled=True)
     gate_rows, query_rows = lax.optimization_barrier((gate_rows, query_rows))
     lowrank = jnp.dot(normed, decay_down, preferred_element_type=jnp.float32).astype(jnp.bfloat16)

time: 398 us -> 365 us (0.917)
  waiting for transfers between devices: 203 us -> 158 us
  local copies, waits for them, and re-layouts: 17 us -> 27.4 us
    all_gather x1, waiting for transfers between devices: 56.9 us -> 24.7 us  [on_device(): down_columns = lax.all_gather(down_weight, 'req', axis=1, tiled=True)]
    all_gather x2 -> x1, waiting for transfers between devices: 99.9 us -> 88.3 us  [on_device(): lax.all_gather(jnp.concatenate([gate_weight, up_weight], axis=1), 'req',...]
    split x0 -> x1, local copies, waits for them, and re-layouts: none -> 9.36 us  [on_device(): jnp.split(lax.all_gather(jnp.concatenate([gate_weight, up_weight], axis=1...]
    unnamed x43 -> x47, local copies, waits for them, and re-layouts: 12.8 us -> 13.8 us
  transfers between devices with their start and end apart: 7 -> 6, of which waited for: 6 -> 5; matrix products, arithmetic and copies ran while one was open for 17% -> 21% of each run, Pallas kernels for 0% -> 0%
where the time goes in v1:
time: 365 us; the launch traced here: 358 us
  waiting for transfers between devices  158 us (43%)
  matrix products  101 us (28%)
  other arithmetic  45.5 us (12%)
  local copies, waits for them, and re-layouts  27.4 us (8%)
  between operations  14.7 us (4%)
  blocking collectives  6.9 us (2%)
  starting transfers between devices  4.57 us (1%)
    all_gather x1, waiting for transfers between devices, on_device(): lax.all_gather(jnp.concatenate([gate_weight, up_weight], axis=1), 'req',...  88.3 us
    psum x1, waiting for transfers between devices, on_device(): lax.psum(partial_value.astype(jnp.bfloat16), 'hid').astype(jnp.float32)  34.2 us
    all_gather x1, waiting for transfers between devices, on_device(): down_columns = lax.all_gather(down_weight, 'req', axis=1, tiled=True)  24.7 us
    dot_general x1, matrix products, on_device(): partials = jnp.dot(hidden, down_columns, preferred_element_type=jnp.float32)  20.9 us
    unnamed x47, local copies, waits for them, and re-layouts  13.8 us
    dot_general x1, matrix products, page_block(): jnp.einsum('phik,phkv->phiv', raised_rows, previous, precision=TOP_PRECIS...  13.7 us
    dot_general x1, matrix products, page_block(): jnp.einsum('pqhe,qheb->pheb', weights, page_terms, precision=TOP_PRECISION)  13.6 us
    dot_general x1, matrix products, widen(): return jnp.dot(feed_in, weight_rows, preferred_element_type=jnp.float32)  10.7 us
  transfers between devices with their start and end apart: 6, of which 5 were waited for; matrix products, arithmetic and copies ran while one was open for 21% of the time, Pallas kernels for 0%

profile of v1, /device:TPU:1, one launch (start us, length us, event | category | flops | bytes accessed | tf_op | source)
XLA Modules:
  0.0 358.4 jit_solution(5242208729086664033)
XLA Ops:
  11.6 7.2 %convolution_convert_fusion.2 = bf16[1024,1024]{1,0:T(8,128)(2,1)S(1)} fusion(bf16[2048,1024]{1,0:T(8,128)(2,1)} %param.20, bf16[1024,2048]{1,0:T(8,128)(2,1)S(1)} %copy-done.7, f32[2048]{0:T(1024)S(1)} %convert_element_type.149, f32[1024]{0:T(1024)S(1)} %add_rsqrt_fusion.2), kind=kOutput, calls=%fused_computation.53 | convolution fusion | flops 4304404480 | bytes 10498048 | tf_op jit(solution)/shard_map/dot_general | solution.py:143
  20.2 4.4 %collective-permute-start = (bf16[3,1024]{1,0:T(4,128)(2,1)S(1)}, bf16[3,1024]{1,0:T(4,128)(2,1)S(1)}, u32[]{:S(2)}, u32[]{:S(2)}) collective-permute-start(bf16[3,1024]{1,0:T(4,128)(2,1)S(1)} %slice_bitcast_fusion.5), channel_id=1, source_target_pairs={{0,2},{2,4},{4,6},{1,3},{3,5},{5,7},{8,10},{10,12},{12,14},{9,11},... | collective-permute-start | bytes 18440 | tf_op jit(solution)/shard_map/ppermute | solution.py:18
  24.7 5.2 %fusion.37 = f32[1024,256]{1,0:T(8,128)} fusion(bf16[16,256]{1,0:T(8,128)(2,1)S(1)} %copy-done.20, bf16[2048,16]{0,1:T(8,128)(2,1)S(1)} %copy-done.19, f32[256]{0:T(256)S(1)} %copy-done.21, bf16[1024,2048]{1,0:T(8,128)(2,1)} %param.18, f32[2048]{0:T(1024)S(1)} %convert_element_type.149, f32[1024]{0:T(1024)S(1)} %add_rsqrt_fusion.2), kind=kOutput, calls=%fused_computation.60 | convolution fusion | flops 86523904 | bytes 5329920 | tf_op jit(solution)/shard_map/dot_general | solution.py:165
  32.3 4.1 %convert_element_type.152 = f32[16,64,1024]{2,1,0:T(8,128)} convert(bf16[16,64,1024]{2,1,0:T(8,128)(2,1)} %bitcast.122) | non-fusion elementwise | flops 1048576 | bytes 6291456 | tf_op jit(solution)/shard_map/convert_element_type | solution.py:63
  37.6 7.7 %fusion.15 = f32[16,64,1,1024]{3,1,0,2:T(8,128)S(1)} fusion(f32[16,64,1024]{2,1,0:T(8,128)} %convert_element_type.152, f32[16,3,1024]{2,1,0:T(4,128)S(1)} %convert_multiply_fusion.4, f32[1024]{0:T(1024)S(1)} %bitcast.130, f32[1024]{0:T(1024)S(1)} %bitcast.131, f32[1024]{0:T(1024)S(1)} %bitcast.129, f32[1024]{0:T(1024)S(1)} %bitcast.128), kind=kLoop, calls=%fused_computation.29 | loop fusion | flops 10485760 | bytes 8601600 | tf_op jit(solution)/shard_map/reshape | solution.py:149
  45.3 7.4 %fusion.30 = f32[16,256,512]{2,1,0:T(8,128)S(1)} fusion(f32[16,64,1,1024]{3,1,0,2:T(8,128)S(1)} %fusion.15, f32[16,1,64,256]{3,0,1,2:T(8,128)S(1)} %fusion.49, f32[16,256]{1,0:T(8,128)S(1)} %get-tuple-element.99), kind=kOutput, calls=%fused_computation.51 | convolution fusion | flops 1612447744 | bytes 12599296 | tf_op jit(solution)/shard_map/phte,phtb->pheb/dot_general | solution.py:99
  52.7 13.6 %fusion.20 = f32[16,1,256,512]{3,0,2,1:T(8,128)S(1)} fusion(f32[16,256,512]{2,1,0:T(8,128)S(1)} %fusion.30, f32[16,256]{0,1:T(8,128)S(1)} %bitcast.125, pred[16,16]{1,0:T(8,128)(4,1)S(1)} %fusion.72), kind=kOutput, calls=%fused_computation.38 | convolution fusion | flops 402849792 | bytes 16793856 | tf_op jit(solution)/shard_map/pqhe,qheb->pheb/dot_general | solution.py:107
  74.0 6.9 %all_gather.16 = bf16[4,1,256]{2,1,0:T(2,128)(2,1)S(1)} all-gather(bf16[1,1,256]{2,1,0:T(2,128)(2,1)S(1)} %fusion.74), channel_id=1, replica_groups=mesh['req'=16,'seq'=4,'hid'=2] {'seq'}, dimensions={0}, use_global_device_ids=true | all-gather | bytes 2560 | tf_op jit(solution)/shard_map/all_gather | solution.py:24
  83.5 8.7 %multiply_bitcast_fusion = f32[16,256,512]{2,0,1:T(8,128)} fusion(f32[15,1,256,512]{3,0,2,1:T(8,128)} %bitcast.119, f32[16]{0:T(128)S(1)} %get-tuple-element.95), kind=kLoop, calls=%fused_computation.19 | loop fusion | flops 2097152 | bytes 16252992 | tf_op jit(solution)/shard_map/reshape.33
  92.2 4.4 %all-gather.8.cloned.1.call-done = bf16[4,1,256,512]{3,2,1,0:T(8,128)(2,1)} async-done(((bf16[1,1,256,512]{3,2,1,0:T(8,128)(2,1)}), bf16[4,1,256,512]{3,2,1,0:T(8,128)(2,1)}) %all-gather.8.cloned.1.call-update) | async-done | bytes 1048592 | tf_op jit(solution)/shard_map/all_gather | solution.py:24
  96.8 88.3 %all-gather.6.cloned.1.call-done = bf16[2048,2816]{1,0:T(8,128)(2,1)} async-done(((bf16[128,2816]{1,0:T(8,128)(2,1)}), bf16[2048,2816]{1,0:T(8,128)(2,1)}) %all-gather.6.cloned.1.call-update) | async-done | bytes 11534352 | tf_op jit(solution)/shard_map/all_gather | solution.py:154
  185.1 9.4 %fusion.88 = (bf16[2048,1408]{1,0:T(8,128)(2,1)}, bf16[2048,1408]{1,0:T(8,128)(2,1)}) fusion(bf16[2048,2816]{1,0:T(8,128)(2,1)} %all-gather.6.cloned.1.call-done), kind=kLoop, calls=%fused_computation.133 | loop fusion | bytes 23068672 | tf_op jit(solution)/shard_map/split | solution.py:153
  194.5 4.8 %convolution_select_fusion = f32[16,64,64]{2,1,0:T(8,128)S(1)} fusion(f32[16,1,64,256]{3,2,0,1:T(8,128)} %multiply_bitcast_fusion.1, f32[16,1,64,256]{3,0,1,2:T(8,128)} %copy-done.5, pred[64,64]{1,0:T(8,128)(4,1)S(1)} %iota_compare_fusion, f32[16,64,1,1024]{3,1,0,2:T(8,128)} %copy-done.3), kind=kOutput, calls=%fused_computation.56 | convolution fusion | flops 203489280 | bytes 4460544 | tf_op jit(solution)/shard_map/phik,phjk->phij/dot_general | solution.py:92
  201.2 13.7 %fusion.7 = f32[16,64,512]{2,1,0:T(8,128)S(1)} fusion(f32[16,256,512]{2,0,1:T(8,128)} %multiply_bitcast_fusion, f32[16,1,64,256]{3,2,0,1:T(8,128)S(1)} %copy-done.8, f32[16,1,64,256]{3,0,1,2:T(8,128)S(1)} %copy-done.6), kind=kOutput, calls=%fused_computation.14 | convolution fusion | flops 1610874880 | bytes 12582912 | tf_op jit(solution)/shard_map/phik,phkv->phiv/dot_general | solution.py:110
  219.1 7.4 %fusion.25 = bf16[1024,512]{1,0:T(8,128)(2,1)} fusion(f32[16,1,64,512]{3,2,0,1:T(8,128)} %copy-done.10, f32[512]{0:T(512)S(1)} %convert_element_type.163, f32[1024]{0:T(1024)S(1)} %rsqrt.29, bf16[2048,512]{1,0:T(8,128)(2,1)} %param.25, bf16[1024,2048]{1,0:T(8,128)(2,1)} %param.18, f32[2048]{0:T(1024)S(1)} %convert_element_type.149, ...), kind=kOutput, calls=%fused_computation.45 | convolution fusion | flops 2160066560 | bytes 9455616 | tf_op jit(solution)/shard_map/dot_general | solution.py:200
  226.6 24.7 %all-gather.4.cloned.1.call-done = bf16[1408,2048]{1,0:T(8,128)(2,1)} async-done(((bf16[1408,128]{1,0:T(8,128)(2,1)}), bf16[1408,2048]{1,0:T(8,128)(2,1)}) %all-gather.4.cloned.1.call-update) | async-done | bytes 5767184 | tf_op jit(solution)/shard_map/all_gather | solution.py:160
  251.2 5.6 %convolution_convert_fusion.1 = bf16[1024,2048]{1,0:T(8,128)(2,1)} fusion(bf16[1024,512]{1,0:T(8,128)(2,1)} %fusion.25, bf16[512,2048]{1,0:T(8,128)(2,1)S(1)} %copy-done), kind=kOutput, calls=%fused_computation.37 | convolution fusion | flops 2149580800 | bytes 7340032 | tf_op jit(solution)/shard_map/dot_general | solution.py:207
  257.5 34.2 %all-reduce.3.cloned.1.call-done = bf16[1024,2048]{1,0:T(8,128)(2,1)} async-done(((bf16[1024,2048]{1,0:T(8,128)(2,1)}), bf16[1024,2048]{1,0:T(8,128)(2,1)}) %all-reduce.3.cloned.1.call-update) | async-done | bytes 4194320 | tf_op jit(solution)/shard_map/psum | solution.py:210
  291.8 5.5 %fusion = (f32[1024]{0:T(1024)S(1)}, bf16[1024,2048]{1,0:T(8,128)(2,1)S(1)}) fusion(bf16[1024,2048]{1,0:T(8,128)(2,1)} %all-reduce.3.cloned.1.call-done, bf16[1024,2048]{1,0:T(8,128)(2,1)} %param.18), kind=kLoop, calls=%fused_computation.7 | loop fusion | flops 14679040 | bytes 12587008 | tf_op jit(solution)/shard_map/reduce_sum | solution.py:45
  299.2 10.7 %fusion.34 = f32[1024,1408]{1,0:T(8,128)} fusion(bf16[2048,1408]{1,0:T(8,128)(2,1)} %get-tuple-element.57, bf16[1024,2048]{1,0:T(8,128)(2,1)S(1)} %get-tuple-element.93, f32[2048]{0:T(1024)S(1)} %convert_element_type.170, f32[1024]{0:T(1024)S(1)} %add_rsqrt_fusion.1), kind=kOutput, calls=%fused_computation.57 | convolution fusion | flops 5913968640 | bytes 15740928 | tf_op jit(solution)/shard_map/dot_general | solution.py:216
  309.9 20.9 %convolution_convert_fusion = bf16[1024,2048]{1,0:T(8,128)(2,1)} fusion(bf16[1408,2048]{1,0:T(8,128)(2,1)} %all-gather.4.cloned.1.call-done, f32[1024,1408]{1,0:T(8,128)} %fusion.34, bf16[2048,1408]{1,0:T(8,128)(2,1)} %get-tuple-element.58, bf16[1024,2048]{1,0:T(8,128)(2,1)} %copy-done.9, f32[2048]{0:T(1024)S(1)} %convert_element_type.170, ...), kind=kOutput, calls=%fused_computation.36 | convolution fusion | flops 11830296576 | bytes 25702400 | tf_op jit(solution)/shard_map/dot_general | solution.py:221
  336.7 4.5 %copy.75 = bf16[16,1,256,512]{3,2,1,0:T(8,128)(2,1)} copy(bf16[16,1,256,512]{3,0,2,1:T(8,128)(2,1)S(1)} %add_convert_fusion) | data formatting | bytes 8388608
  341.2 5.8 %reduce-scatter.2.cloned.1.call-done = bf16[512,2048]{1,0:T(8,128)(2,1)} async-done(((bf16[1024,2048]{1,0:T(8,128)(2,1)}), bf16[512,2048]{1,0:T(8,128)(2,1)}) %reduce-scatter.2.cloned.1.call-update) | async-done | bytes 2097168 | tf_op jit(solution)/shard_map/reduce_scatter | solution.py:222
  347.0 4.4 %add_convert_fusion.1 = bf16[512,2048]{1,0:T(8,128)(2,1)} fusion(bf16[512,2048]{1,0:T(8,128)(2,1)} %reduce-scatter.2.cloned.1.call-done, bf16[1024,2048]{1,0:T(8,128)(2,1)} %copy-done.9, s32[]{:T(128)S(6)} %select_n.46), kind=kLoop, calls=%fused_computation.35 | loop fusion | flops 4194304 | bytes 6291460 | tf_op jit(solution)/shard_map/convert_element_type | solution.py:225
  (101 shorter events, 34.3 us)
Async XLA Ops:
  7.2 244.1 %copy-start = (bf16[512,2048]{1,0:T(8,128)(2,1)S(1)}, bf16[512,2048]{1,0:T(8,128)(2,1)}, u32[]{:S(2)}) copy-start(bf16[512,2048]{1,0:T(8,128)(2,1)} %param.27) | copy-start | bytes 6291460
  7.2 89.4 %all-gather.8.cloned.1.call-start = ((), (), s32[]{:S(2)}) async-start(), calls=%async_computation.3 | async-start | bytes 1310720 | tf_op jit(solution)/shard_map/all_gather | solution.py:24
  7.2 4.3 %copy-start.7 = (bf16[1024,2048]{1,0:T(8,128)(2,1)S(1)}, bf16[1024,2048]{1,0:T(8,128)(2,1)}, u32[]{:S(2)}) copy-start(bf16[1024,2048]{1,0:T(8,128)(2,1)} %param.18) | copy-start | bytes 12582916
  11.5 13.0 %copy-start.16 = (s32[1,16]{1,0:T(1,128)S(1)}, s32[1,16]{1,0:T(1,128)}, u32[]{:S(2)}) copy-start(s32[1,16]{1,0:T(1,128)} %param.33) | copy-start | bytes 196
  11.5 13.0 %copy-start.18 = (s32[1,16]{1,0:T(1,128)S(1)}, s32[1,16]{1,0:T(1,128)}, u32[]{:S(2)}) copy-start(s32[1,16]{1,0:T(1,128)} %param.32) | copy-start | bytes 196
  11.5 13.2 %copy-start.14 = (bf16[4,1024]{1,0:T(4,128)(2,1)S(1)}, bf16[4,1024]{1,0:T(4,128)(2,1)}, u32[]{:S(2)}) copy-start(bf16[4,1024]{1,0:T(4,128)(2,1)} %param.21) | copy-start | bytes 24580
  11.5 13.2 %copy-start.19 = (bf16[2048,16]{0,1:T(8,128)(2,1)S(1)}, bf16[2048,16]{0,1:T(8,128)(2,1)}, u32[]{:S(2)}) copy-start(bf16[2048,16]{0,1:T(8,128)(2,1)} %param.22) | copy-start | bytes 196612
  11.5 13.2 %copy-start.20 = (bf16[16,256]{1,0:T(8,128)(2,1)S(1)}, bf16[16,256]{1,0:T(8,128)(2,1)}, u32[]{:S(2)}) copy-start(bf16[16,256]{1,0:T(8,128)(2,1)} %param.23) | copy-start | bytes 24580
  11.6 13.2 %copy-start.21 = (f32[256]{0:T(256)S(1)}, f32[256]{0:T(256)}, u32[]{:S(2)}) copy-start(f32[256]{0:T(256)} %param.24) | copy-start | bytes 3076
  20.2 17.3 %collective-permute-start = (bf16[3,1024]{1,0:T(4,128)(2,1)S(1)}, bf16[3,1024]{1,0:T(4,128)(2,1)S(1)}, u32[]{:S(2)}, u32[]{:S(2)}) collective-permute-start(bf16[3,1024]{1,0:T(4,128)(2,1)S(1)} %slice_bitcast_fusion.5), channel_id=1, source_target_pairs={{0,2},{2,4},{4,6},{1,3},{3,5},{5,7},{8,10},{10,12},{12,14},{9,11},... | collective-permute-start | bytes 18440 | tf_op jit(solution)/shard_map/ppermute | solution.py:18
  31.8 13.5 %copy-start.5 = (f32[16,1,64,256]{3,0,1,2:T(8,128)}, f32[16,1,64,256]{3,0,1,2:T(8,128)S(1)}, u32[]{:S(2)}) copy-start(f32[16,1,64,256]{3,0,1,2:T(8,128)S(1)} %fusion.49) | copy-start | bytes 3145732
  45.3 7.4 %copy-start.3 = (f32[16,64,1,1024]{3,1,0,2:T(8,128)}, f32[16,64,1,1024]{3,1,0,2:T(8,128)S(1)}, u32[]{:S(2)}) copy-start(f32[16,64,1,1024]{3,1,0,2:T(8,128)S(1)} %fusion.15) | copy-start | bytes 12582916
  52.7 18.3 %copy-start.12 = (bf16[128,1408]{1,0:T(8,128)(2,1)S(1)}, bf16[128,1408]{1,0:T(8,128)(2,1)}, u32[]{:S(2)}) copy-start(bf16[128,1408]{1,0:T(8,128)(2,1)} %param.30) | copy-start | bytes 1081348
  52.7 18.3 %copy-start.13 = (bf16[128,1408]{1,0:T(8,128)(2,1)S(1)}, bf16[128,1408]{1,0:T(8,128)(2,1)}, u32[]{:S(2)}) copy-start(bf16[128,1408]{1,0:T(8,128)(2,1)} %param.29) | copy-start | bytes 1081348
  66.3 3.3 copy-start.2
  69.6 3.9 %copy-start.17 = (bf16[512]{0:T(512)(128)(2,1)S(1)}, bf16[512]{0:T(512)(128)(2,1)}, u32[]{:S(2)}) copy-start(bf16[512]{0:T(512)(128)(2,1)} %param.26) | copy-start | bytes 3076
  70.9 114.2 %all-gather.6.cloned.1.call-start = ((), (), s32[]{:S(2)}) async-start(), calls=%async_computation.2 | async-start | bytes 12255232 | tf_op jit(solution)/shard_map/all_gather | solution.py:154
  71.9 179.3 %all-gather.4.cloned.1.call-start = ((), (), s32[]{:S(2)}) async-start(), calls=%async_computation.1 | async-start | bytes 6127616 | tf_op jit(solution)/shard_map/all_gather | solution.py:160
  72.7 219.1 %all-reduce.3.cloned.1.call-start = ((), (), s32[]{:S(2)}) async-start(), calls=%async_computation.4 | async-start | bytes 8388608 | tf_op jit(solution)/shard_map/psum | solution.py:210
  194.5 4.8 %copy-start.4 = (f32[16,64,1,1024]{3,1,0,2:T(8,128)S(1)}, f32[16,64,1,1024]{3,1,0,2:T(8,128)}, u32[]{:S(2)}) copy-start(f32[16,64,1,1024]{3,1,0,2:T(8,128)} %copy-done.3) | copy-start | bytes 12582916
  194.5 6.7 %copy-start.6 = (f32[16,1,64,256]{3,0,1,2:T(8,128)S(1)}, f32[16,1,64,256]{3,0,1,2:T(8,128)}, u32[]{:S(2)}) copy-start(f32[16,1,64,256]{3,0,1,2:T(8,128)} %copy-done.5) | copy-start | bytes 3145732
  194.5 6.7 %copy-start.8 = (f32[16,1,64,256]{3,2,0,1:T(8,128)S(1)}, f32[16,1,64,256]{3,2,0,1:T(8,128)}, u32[]{:S(2)}) copy-start(f32[16,1,64,256]{3,2,0,1:T(8,128)} %multiply_bitcast_fusion.1) | copy-start | bytes 3145732
  256.8 90.2 %reduce-scatter.2.cloned.1.call-start = ((), (), s32[]{:S(2)}) async-start(), calls=%async_computation.5 | async-start | bytes 6291456 | tf_op jit(solution)/shard_map/reduce_scatter | solution.py:222
  336.7 14.8 %copy-start.1 = (bf16[512,2048]{1,0:T(8,128)(2,1)S(1)}, bf16[512,2048]{1,0:T(8,128)(2,1)}, u32[]{:S(2)}) copy-start(bf16[512,2048]{1,0:T(8,128)(2,1)} %param.27) | copy-start | bytes 6291460
  (4 other events, 5.3 us)
Sparse Core Ops, SparseCore 0:
  71.0 25.4 all-gather.7
  98.7 86.3 all-gather.5
  187.3 63.9 all-gather.3
  257.0 34.7 all-reduce.2
  330.9 16.0 reduce-scatter.1
